TPU v7x, 256 devices: a whole 4x4x8 slice. The times are simulated.
256 devices in a mesh: wide: 32 (over z, y), narrow: 8 (over x, core).
Axes of the slice: x: 4, y: 4, z: 8, core: 2. Of those that a mesh axis runs over, the one named last changes fastest.
Arguments:
- blocks: float32 [8192, 8, 64, 64], P(('wide', 'narrow'))
- col_index: int32 [8192, 8], P(('wide', 'narrow')), may hold values from 0 to 8191, as said below
- right_side: float32 [16, 524288], P(None, ('wide', 'narrow')), may hold values from -6 to 6
- start_guess: float32 [16, 524288], P(None, ('wide', 'narrow')), may hold values from -3 to 3
Outputs:
- new_guess: float32 [16, 524288], P(None, ('wide', 'narrow'))
- new_residual: float32 [16, 524288], P(None, ('wide', 'narrow'))
Inputs may be any that keep to these rules, and one draw needn't show every extreme that they name: col_index[g, 0] = g; the other entries of row g are distinct and differ from g, each at most 8 block rows away from g counted circularly over 8192 block rows.
All inputs are finite; a program needn't handle non-finite values.
Results may differ from a plain program's by a relative error of at most 0.0003.
Values sent between devices are 32-bit elements; how exact they have to be, the bound alone decides.
A program may use at most 64 MiB of HBM per device.

v0:
```python
import jax
import jax.numpy as jnp
from jax import lax
from jax.sharding import Mesh
from jax.sharding import PartitionSpec as P

S = 4
BAND = 8
WIDE_NARROW = ("wide_0", "wide_1", "narrow_0", "narrow_1")


def with_halo(array, sides, width):
    edges = {}
    for axis, dim in sides:
        peers, length = (lax.axis_size(axis), array.shape[dim])
        up = [(i, (i + 1) % peers) for i in range(peers)]
        last = lax.slice_in_dim(array, length - width, length, axis=dim)
        first = lax.slice_in_dim(array, 0, width, axis=dim)
        edges[dim] = (
            lax.ppermute(last, axis, up),
            lax.ppermute(first, axis, [(b, a) for a, b in up]),
        )
    done = []
    for _, dim in sides:
        low, high = edges[dim]
        around = [(width, width) if d in done else (0, 0) for d in range(array.ndim)]
        array = jnp.concatenate([jnp.pad(low, around), array, jnp.pad(high, around)], axis=dim)
        done.append(dim)
    return array


def one_axis_at_a_time(array, axes):
    for axis in axes:
        array = lax.psum(array, axis)
    return array


def extend_vector(vec, rows):
    cells = vec.shape[1] // rows
    depth = BAND
    extended = with_halo(vec, ((WIDE_NARROW, 1),), BAND * cells)
    return (extended, depth)


def apply_matrix(vec, blocks, col_index):
    rows = blocks.shape[0]
    cells = blocks.shape[2]
    nrhs = vec.shape[0]
    extended, depth = extend_vector(vec, rows)
    total_rows = rows * lax.axis_size(WIDE_NARROW)
    first_row = lax.axis_index(WIDE_NARROW) * rows
    relative = (col_index - first_row + BAND + total_rows) % total_rows
    position = relative - BAND + depth
    shaped = extended.reshape(nrhs, extended.shape[1] // cells, cells)
    picked = jnp.take(shaped, position, axis=1)
    result = jnp.einsum("irkb,rkab->ira", picked, blocks, precision=lax.Precision.HIGHEST)
    return result.reshape(nrhs, rows * cells)


def per_device(blocks, col_index, right_side, start_guess):
    hp = lax.Precision.HIGHEST
    nrhs = right_side.shape[0]
    residual = right_side - apply_matrix(start_guess, blocks, col_index)
    vectors = [residual]
    for step in range(S - 1):
        vectors.append(apply_matrix(vectors[-1], blocks, col_index) - 2.0 * vectors[-1])
    basis = jnp.concatenate(vectors, axis=0)
    local_gram = jnp.dot(basis, basis.T, precision=hp)
    gram = one_axis_at_a_time(local_gram, WIDE_NARROW)
    upper = jnp.linalg.cholesky(gram).T
    lower_cols = (S - 1) * nrhs
    hess = upper[:, nrhs:] + 2.0 * upper[:, :lower_cols]
    normal = jnp.dot(hess.T, hess, precision=hp)
    target = jnp.dot(hess.T, upper[:, :nrhs], precision=hp)
    factor = jnp.linalg.cholesky(normal)
    middle = lax.linalg.triangular_solve(factor, target, left_side=True, lower=True)
    coeff = lax.linalg.triangular_solve(
        factor, middle, left_side=True, lower=True, transpose_a=True
    )
    low_part = basis[:lower_cols]
    high_part = basis[nrhs:] + 2.0 * low_part
    new_guess = start_guess + jnp.dot(coeff.T, low_part, precision=hp)
    new_residual = residual - jnp.dot(coeff.T, high_part, precision=hp)
    return (new_guess, new_residual)


def solution(mesh):
    torus = Mesh(mesh.devices.reshape(8, 4, 4, 2), ("wide_0", "wide_1", "narrow_0", "narrow_1"))
    in_specs = (
        P(WIDE_NARROW, None, None, None),
        P(WIDE_NARROW, None),
        P(None, WIDE_NARROW),
        P(None, WIDE_NARROW),
    )
    out_specs = (P(None, WIDE_NARROW), P(None, WIDE_NARROW))
    return jax.shard_map(
        per_device, mesh=torus, in_specs=in_specs, out_specs=out_specs, check_vma=False
    )
```

profile of v0, /device:TPU:1, one launch (start us, length us, event | category | flops | bytes accessed | tf_op | source)
XLA Modules:
  0.0 166.4 jit_solution(17623749729161626469)
XLA Ops:
  0.6 0.8 fusion.73
  1.4 2.6 %collective-permute-start = (f32[16,512]{1,0:T(8,128)S(1)}, f32[16,512]{1,0:T(8,128)S(1)}, u32[]{:S(2)}, u32[]{:S(2)}) collective-permute-start(f32[16,512]{1,0:T(8,128)S(1)} %get-tuple-element.11), channel_id=1, source_target_pairs={{0,1},{1,2},{2,3},{3,4},{4,5},{5,6},{6,7},{7,8},{8,9},{9,10},{10,1... | collective-permute-start | bytes 98312 | tf_op jit(solution)/shard_map/ppermute | solution.py:20
  4.0 0.7 collective-permute-start.1
  4.7 0.7 compare_and_fusion
  5.7 1.6 collective-permute-done.1
  7.4 0.9 pad_maximum_fusion.3
  8.5 1.0 gather_fusion
  9.6 9.4 %fusion.12 = f32[16,32,64]{2,0,1:T(8,128)S(1)} fusion(f32[32,8,64,64]{3,2,1,0:T(8,128)} %param.6, f32[32,8,16,64]{3,2,1,0:T(8,128)S(1)} %bitcast.70, pred[32,8]{1,0:T(8,128)(4,1)S(1)} %copy.35), kind=kOutput, calls=%fused_computation.18 | convolution fusion | flops 201588736 | bytes 5374208 | tf_op jit(solution)/shard_map/irkb,rkab->ira/dot_general | solution.py:56
  19.3 7.3 %collective-permute-start.3 = (f32[16,512]{1,0:T(8,128)S(1)}, f32[16,512]{1,0:T(8,128)S(1)}, u32[]{:S(2)}, u32[]{:S(2)}) collective-permute-start(f32[16,512]{1,0:T(8,128)S(1)} %get-tuple-element.10), channel_id=1, source_target_pairs={{1,0},{2,1},{3,2},{4,3},{5,4},{6,5},{7,6},{8,7},{9,8},{10,9},{11,1... | collective-permute-start | bytes 98312 | tf_op jit(solution)/shard_map/ppermute | solution.py:21
  26.6 0.6 collective-permute-done.2
  27.7 1.0 gather_fusion.1
  28.7 9.3 %fusion.15 = f32[16,32,64]{2,0,1:T(8,128)S(1)} fusion(f32[32,8,64,64]{3,2,1,0:T(8,128)} %param.6, f32[32,8,16,64]{3,2,1,0:T(8,128)S(1)} %bitcast.71, pred[32,8]{1,0:T(8,128)(4,1)S(1)} %copy.35), kind=kOutput, calls=%fused_computation.19 | convolution fusion | flops 201588736 | bytes 5374208 | tf_op jit(solution)/shard_map/irkb,rkab->ira/dot_general | solution.py:56
  38.6 8.0 %collective-permute-start.5 = (f32[16,512]{1,0:T(8,128)S(1)}, f32[16,512]{1,0:T(8,128)S(1)}, u32[]{:S(2)}, u32[]{:S(2)}) collective-permute-start(f32[16,512]{1,0:T(8,128)S(1)} %get-tuple-element.8), channel_id=1, source_target_pairs={{1,0},{2,1},{3,2},{4,3},{5,4},{6,5},{7,6},{8,7},{9,8},{10,9},{11,1... | collective-permute-start | bytes 98312 | tf_op jit(solution)/shard_map/ppermute | solution.py:21
  46.6 0.6 collective-permute-done.4
  47.7 1.0 gather_fusion.2
  48.7 9.3 %fusion.18 = f32[16,32,64]{2,0,1:T(8,128)S(1)} fusion(f32[32,8,64,64]{3,2,1,0:T(8,128)} %param.6, f32[32,8,16,64]{3,2,1,0:T(8,128)S(1)} %bitcast.72, pred[32,8]{1,0:T(8,128)(4,1)S(1)} %copy.35), kind=kOutput, calls=%fused_computation.20 | convolution fusion | flops 201588736 | bytes 5374208 | tf_op jit(solution)/shard_map/irkb,rkab->ira/dot_general | solution.py:56
  58.4 8.0 %collective-permute-start.7 = (f32[16,512]{1,0:T(8,128)S(1)}, f32[16,512]{1,0:T(8,128)S(1)}, u32[]{:S(2)}, u32[]{:S(2)}) collective-permute-start(f32[16,512]{1,0:T(8,128)S(1)} %get-tuple-element.6), channel_id=1, source_target_pairs={{1,0},{2,1},{3,2},{4,3},{5,4},{6,5},{7,6},{8,7},{9,8},{10,9},{11,1... | collective-permute-start | bytes 98312 | tf_op jit(solution)/shard_map/ppermute | solution.py:21
  67.5 1.0 gather_fusion.3
  68.5 9.3 %fusion.21 = f32[16,32,64]{2,0,1:T(8,128)S(1)} fusion(f32[32,8,64,64]{3,2,1,0:T(8,128)} %param.6, f32[32,8,16,64]{3,2,1,0:T(8,128)S(1)} %bitcast.69, pred[32,8]{1,0:T(8,128)(4,1)S(1)} %copy.35), kind=kOutput, calls=%fused_computation.21 | convolution fusion | flops 201588736 | bytes 5374208 | tf_op jit(solution)/shard_map/irkb,rkab->ira/dot_general | solution.py:56
  78.7 20.1 %psum.28 = f32[64,64]{0,1:T(8,128)S(1)} all-reduce(f32[64,64]{0,1:T(8,128)S(1)} %fusion.32), channel_id=1, replica_groups=mesh['wide_0'=8,'wide_1'=4,'narrow_0'=4,'narrow_1'=2] {'wide_0'}, use_global_device_ids=true, to_apply=%region_0.2 | all-reduce | flops 4096 | bytes 32768 | tf_op jit(solution)/shard_map/psum | solution.py:34
  98.8 10.9 %psum.29 = f32[64,64]{0,1:T(8,128)S(1)} all-reduce(f32[64,64]{0,1:T(8,128)S(1)} %psum.28), channel_id=1, replica_groups=mesh['wide_0'=8,'wide_1'=4,'narrow_0'=4,'narrow_1'=2] {'wide_1'}, use_global_device_ids=true, to_apply=%region_1.3 | all-reduce | flops 4096 | bytes 32768 | tf_op jit(solution)/shard_map/psum | solution.py:34
  109.7 26.0 %psum.30 = f32[64,64]{0,1:T(8,128)S(1)} all-reduce(f32[64,64]{0,1:T(8,128)S(1)} %psum.29), channel_id=1, replica_groups=mesh['wide_0'=8,'wide_1'=4,'narrow_0'=4,'narrow_1'=2] {'narrow_0'}, use_global_device_ids=true, to_apply=%region_2.4 | all-reduce | flops 4096 | bytes 32768 | tf_op jit(solution)/shard_map/psum | solution.py:34
  135.8 11.2 %psum.31 = f32[64,64]{0,1:T(8,128)S(1)} all-reduce(f32[64,64]{0,1:T(8,128)S(1)} %psum.30), channel_id=1, replica_groups=mesh['wide_0'=8,'wide_1'=4,'narrow_0'=4,'narrow_1'=2] {'narrow_1'}, use_global_device_ids=true, to_apply=%region_3.5 | all-reduce | flops 4096 | bytes 32768 | tf_op jit(solution)/shard_map/psum | solution.py:34
  147.1 5.8 %cholesky.34 = f32[64,64]{1,0:T(8,128)S(1)} custom-call(f32[64,64]{1,0:T(8,128)S(1)} %fusion.46), custom_call_target="Cholesky" | custom-call | tf_op jit(solution)/shard_map/jit(cholesky)/cholesky | solution.py:70
  153.0 0.6 compare_reduce_fusion.1
  153.6 0.7 select_bitcast_fusion
  154.7 4.4 %cholesky.64 = f32[48,48]{1,0:T(8,128)S(1)} custom-call(f32[48,48]{1,0:T(8,128)S(1)} %fusion.53), custom_call_target="Cholesky" | custom-call | tf_op jit(solution)/shard_map/jit(cholesky)/cholesky | solution.py:75
  159.1 0.6 compare_reduce_fusion
  159.8 0.7 fusion.47
  160.4 3.7 %custom-call.11 = f32[1,48,48]{1,2,0:T(8,128)S(1)} custom-call(f32[1,48,48]{2,1,0:T(8,128)S(1)} %fusion.47), custom_call_target="InvertDiagBlocksLowerTriangular" | custom-call | tf_op jit(solution)/shard_map/triangular_solve | solution.py:77
  164.4 1.0 convolution_subtract_fusion
  165.4 1.0 convolution_add_fusion
  (53 shorter events, 5.5 us)
Async XLA Ops:
  1.4 4.3 %collective-permute-start = (f32[16,512]{1,0:T(8,128)S(1)}, f32[16,512]{1,0:T(8,128)S(1)}, u32[]{:S(2)}, u32[]{:S(2)}) collective-permute-start(f32[16,512]{1,0:T(8,128)S(1)} %get-tuple-element.11), channel_id=1, source_target_pairs={{0,1},{1,2},{2,3},{3,4},{4,5},{5,6},{6,7},{7,8},{8,9},{9,10},{10,1... | collective-permute-start | bytes 98312 | tf_op jit(solution)/shard_map/ppermute | solution.py:20
  4.0 3.3 %collective-permute-start.1 = (f32[16,512]{1,0:T(8,128)S(1)}, f32[16,512]{1,0:T(8,128)S(1)}, u32[]{:S(2)}, u32[]{:S(2)}) collective-permute-start(f32[16,512]{1,0:T(8,128)S(1)} %get-tuple-element.12), channel_id=1, source_target_pairs={{1,0},{2,1},{3,2},{4,3},{5,4},{6,5},{7,6},{8,7},{9,8},{10,9},{11,1... | collective-permute-start | bytes 98312 | tf_op jit(solution)/shard_map/ppermute | solution.py:21
  9.6 9.6 %copy-start.1 = (f32[16,2048]{1,0:T(8,128)S(1)}, f32[16,2048]{1,0:T(8,128)}, u32[]{:S(2)}) copy-start(f32[16,2048]{1,0:T(8,128)} %param.8) | copy-start | bytes 393220
  19.2 8.0 %collective-permute-start.2 = (f32[16,512]{1,0:T(8,128)S(1)}, f32[16,512]{1,0:T(8,128)S(1)}, u32[]{:S(2)}, u32[]{:S(2)}) collective-permute-start(f32[16,512]{1,0:T(8,128)S(1)} %get-tuple-element.9), channel_id=1, source_target_pairs={{0,1},{1,2},{2,3},{3,4},{4,5},{5,6},{6,7},{7,8},{8,9},{9,10},{10,1... | collective-permute-start | bytes 98312 | tf_op jit(solution)/shard_map/ppermute | solution.py:20
  19.3 8.1 %collective-permute-start.3 = (f32[16,512]{1,0:T(8,128)S(1)}, f32[16,512]{1,0:T(8,128)S(1)}, u32[]{:S(2)}, u32[]{:S(2)}) collective-permute-start(f32[16,512]{1,0:T(8,128)S(1)} %get-tuple-element.10), channel_id=1, source_target_pairs={{1,0},{2,1},{3,2},{4,3},{5,4},{6,5},{7,6},{8,7},{9,8},{10,9},{11,1... | collective-permute-start | bytes 98312 | tf_op jit(solution)/shard_map/ppermute | solution.py:21
  38.3 8.9 %collective-permute-start.4 = (f32[16,512]{1,0:T(8,128)S(1)}, f32[16,512]{1,0:T(8,128)S(1)}, u32[]{:S(2)}, u32[]{:S(2)}) collective-permute-start(f32[16,512]{1,0:T(8,128)S(1)} %get-tuple-element.7), channel_id=1, source_target_pairs={{0,1},{1,2},{2,3},{3,4},{4,5},{5,6},{6,7},{7,8},{8,9},{9,10},{10,1... | collective-permute-start | bytes 98312 | tf_op jit(solution)/shard_map/ppermute | solution.py:20
  38.6 8.8 %collective-permute-start.5 = (f32[16,512]{1,0:T(8,128)S(1)}, f32[16,512]{1,0:T(8,128)S(1)}, u32[]{:S(2)}, u32[]{:S(2)}) collective-permute-start(f32[16,512]{1,0:T(8,128)S(1)} %get-tuple-element.8), channel_id=1, source_target_pairs={{1,0},{2,1},{3,2},{4,3},{5,4},{6,5},{7,6},{8,7},{9,8},{10,9},{11,1... | collective-permute-start | bytes 98312 | tf_op jit(solution)/shard_map/ppermute | solution.py:21
  58.3 8.7 %collective-permute-start.6 = (f32[16,512]{1,0:T(8,128)S(1)}, f32[16,512]{1,0:T(8,128)S(1)}, u32[]{:S(2)}, u32[]{:S(2)}) collective-permute-start(f32[16,512]{1,0:T(8,128)S(1)} %get-tuple-element.5), channel_id=1, source_target_pairs={{0,1},{1,2},{2,3},{3,4},{4,5},{5,6},{6,7},{7,8},{8,9},{9,10},{10,1... | collective-permute-start | bytes 98312 | tf_op jit(solution)/shard_map/ppermute | solution.py:20
  58.4 8.8 %collective-permute-start.7 = (f32[16,512]{1,0:T(8,128)S(1)}, f32[16,512]{1,0:T(8,128)S(1)}, u32[]{:S(2)}, u32[]{:S(2)}) collective-permute-start(f32[16,512]{1,0:T(8,128)S(1)} %get-tuple-element.6), channel_id=1, source_target_pairs={{1,0},{2,1},{3,2},{4,3},{5,4},{6,5},{7,6},{8,7},{9,8},{10,9},{11,1... | collective-permute-start | bytes 98312 | tf_op jit(solution)/shard_map/ppermute | solution.py:21
  78.0 87.5 %copy-start = (f32[16,2048]{1,0:T(8,128)S(1)}, f32[16,2048]{1,0:T(8,128)}, u32[]{:S(2)}) copy-start(f32[16,2048]{1,0:T(8,128)} %param.9) | copy-start | bytes 393220
where the time goes:
time: 167 us; the launch traced here: 166 us
  blocking collectives  68.3 us (41%)
  matrix products  40.5 us (24%)
  starting transfers between devices  27 us (16%)
  other arithmetic  18.3 us (11%)
  local copies, waits for them, and re-layouts  7.13 us (4%)
  waiting for transfers between devices  4.22 us (3%)
    psum x4, blocking collectives, one_axis_at_a_time(): array = lax.psum(array, axis)  68.3 us
    dot_general x4, matrix products, apply_matrix(): jnp.einsum('irkb,rkab->ira', picked, blocks, precision=lax.Precision.HIGH...  37.3 us
    ppermute x4, starting transfers between devices, with_halo(): lax.ppermute(first, axis, [(b, a) for a, b in up])  24 us
    another operation x3, other arithmetic, per_device(): upper = jnp.linalg.cholesky(gram).T  6.52 us
    another operation x3, other arithmetic, per_device(): factor = jnp.linalg.cholesky(normal)  5.05 us
    another operation x2, other arithmetic, per_device(): lax.linalg.triangular_solve(factor, middle, left_side=True, lower=True, t...  4.32 us
    gather x4, local copies, waits for them, and re-layouts, apply_matrix(): picked = jnp.take(shaped, position, axis=1)  4.07 us
  transfers between devices with their start and end apart: 8, of which 7 were waited for; matrix products, arithmetic and copies ran while one was open for 1% of the time, Pallas kernels for 0%

commit v1 on v0

--- a/solution.py
+++ b/solution.py
@@ -31,7 +31,7 @@
 
 def one_axis_at_a_time(array, axes):
     for axis in axes:
-        array = lax.psum(array, axis)
+        array = jnp.sum(lax.all_gather(array, axis), axis=0)
     return array
 
 

time: 167 us -> 157 us (0.940)
  blocking collectives: 68.3 us -> 58.4 us
    psum x4 -> x0, blocking collectives: 68.3 us -> none  [one_axis_at_a_time(): array = lax.psum(array, axis)]
    all_gather x0 -> x4, blocking collectives: none -> 58.4 us  [one_axis_at_a_time(): array = jnp.sum(lax.all_gather(array, axis), axis=0)]
where the time goes in v1:
time: 157 us
  blocking collectives  58.4 us (37%)
  matrix products  40.5 us (26%)
  starting transfers between devices  27 us (17%)
  other arithmetic  18.4 us (12%)
  local copies, waits for them, and re-layouts  7.13 us (5%)
  waiting for transfers between devices  4.22 us (3%)
    all_gather x4, blocking collectives, one_axis_at_a_time(): array = jnp.sum(lax.all_gather(array, axis), axis=0)  58.4 us
    dot_general x4, matrix products, apply_matrix(): jnp.einsum('irkb,rkab->ira', picked, blocks, precision=lax.Precision.HIGH...  37.3 us
    ppermute x4, starting transfers between devices, with_halo(): lax.ppermute(first, axis, [(b, a) for a, b in up])  24 us
    another operation x3, other arithmetic, per_device(): upper = jnp.linalg.cholesky(gram).T  6.52 us
    another operation x3, other arithmetic, per_device(): factor = jnp.linalg.cholesky(normal)  5.05 us
    another operation x2, other arithmetic, per_device(): lax.linalg.triangular_solve(factor, middle, left_side=True, lower=True, t...  4.32 us
    gather x4, local copies, waits for them, and re-layouts, apply_matrix(): picked = jnp.take(shaped, position, axis=1)  4.07 us
  transfers between devices with their start and end apart: 8, of which 7 were waited for; matrix products, arithmetic and copies ran while one was open for 1% of the time, Pallas kernels for 0%

profile of v1, /device:TPU:1, one launch (start us, length us, event | category | flops | bytes accessed | tf_op | source)
XLA Modules:
  0.0 156.6 jit_solution(12096292473949543107)
XLA Ops:
  0.6 0.8 fusion.73
  1.4 2.6 %collective-permute-start = (f32[16,512]{1,0:T(8,128)S(1)}, f32[16,512]{1,0:T(8,128)S(1)}, u32[]{:S(2)}, u32[]{:S(2)}) collective-permute-start(f32[16,512]{1,0:T(8,128)S(1)} %get-tuple-element.11), channel_id=1, source_target_pairs={{0,1},{1,2},{2,3},{3,4},{4,5},{5,6},{6,7},{7,8},{8,9},{9,10},{10,1... | collective-permute-start | bytes 98312 | tf_op jit(solution)/shard_map/ppermute | solution.py:20
  4.0 0.7 collective-permute-start.1
  4.7 0.7 compare_and_fusion
  5.7 1.6 %collective-permute-done.1 = f32[16,512]{1,0:T(8,128)S(1)} collective-permute-done((f32[16,512]{1,0:T(8,128)S(1)}, f32[16,512]{1,0:T(8,128)S(1)}, u32[]{:S(2)}, u32[]{:S(2)}) %collective-permute-start.1) | collective-permute-done | bytes 32800 | tf_op jit(solution)/shard_map/ppermute | solution.py:21
  7.4 0.9 pad_maximum_fusion.3
  8.5 1.0 gather_fusion
  9.6 9.4 %fusion.12 = f32[16,32,64]{2,0,1:T(8,128)S(1)} fusion(f32[32,8,64,64]{3,2,1,0:T(8,128)} %param.6, f32[32,8,16,64]{3,2,1,0:T(8,128)S(1)} %bitcast.74, pred[32,8]{1,0:T(8,128)(4,1)S(1)} %copy.51), kind=kOutput, calls=%fused_computation.18 | convolution fusion | flops 201588736 | bytes 5374208 | tf_op jit(solution)/shard_map/irkb,rkab->ira/dot_general | solution.py:56
  19.3 7.3 %collective-permute-start.3 = (f32[16,512]{1,0:T(8,128)S(1)}, f32[16,512]{1,0:T(8,128)S(1)}, u32[]{:S(2)}, u32[]{:S(2)}) collective-permute-start(f32[16,512]{1,0:T(8,128)S(1)} %get-tuple-element.10), channel_id=1, source_target_pairs={{1,0},{2,1},{3,2},{4,3},{5,4},{6,5},{7,6},{8,7},{9,8},{10,9},{11,1... | collective-permute-start | bytes 98312 | tf_op jit(solution)/shard_map/ppermute | solution.py:21
  26.6 0.6 collective-permute-done.2
  27.7 1.0 gather_fusion.1
  28.7 9.3 %fusion.15 = f32[16,32,64]{2,0,1:T(8,128)S(1)} fusion(f32[32,8,64,64]{3,2,1,0:T(8,128)} %param.6, f32[32,8,16,64]{3,2,1,0:T(8,128)S(1)} %bitcast.75, pred[32,8]{1,0:T(8,128)(4,1)S(1)} %copy.51), kind=kOutput, calls=%fused_computation.19 | convolution fusion | flops 201588736 | bytes 5374208 | tf_op jit(solution)/shard_map/irkb,rkab->ira/dot_general | solution.py:56
  38.6 8.0 %collective-permute-start.5 = (f32[16,512]{1,0:T(8,128)S(1)}, f32[16,512]{1,0:T(8,128)S(1)}, u32[]{:S(2)}, u32[]{:S(2)}) collective-permute-start(f32[16,512]{1,0:T(8,128)S(1)} %get-tuple-element.8), channel_id=1, source_target_pairs={{1,0},{2,1},{3,2},{4,3},{5,4},{6,5},{7,6},{8,7},{9,8},{10,9},{11,1... | collective-permute-start | bytes 98312 | tf_op jit(solution)/shard_map/ppermute | solution.py:21
  46.6 0.6 collective-permute-done.4
  47.7 1.0 gather_fusion.2
  48.7 9.3 %fusion.18 = f32[16,32,64]{2,0,1:T(8,128)S(1)} fusion(f32[32,8,64,64]{3,2,1,0:T(8,128)} %param.6, f32[32,8,16,64]{3,2,1,0:T(8,128)S(1)} %bitcast.76, pred[32,8]{1,0:T(8,128)(4,1)S(1)} %copy.51), kind=kOutput, calls=%fused_computation.20 | convolution fusion | flops 201588736 | bytes 5374208 | tf_op jit(solution)/shard_map/irkb,rkab->ira/dot_general | solution.py:56
  58.4 8.0 %collective-permute-start.7 = (f32[16,512]{1,0:T(8,128)S(1)}, f32[16,512]{1,0:T(8,128)S(1)}, u32[]{:S(2)}, u32[]{:S(2)}) collective-permute-start(f32[16,512]{1,0:T(8,128)S(1)} %get-tuple-element.6), channel_id=1, source_target_pairs={{1,0},{2,1},{3,2},{4,3},{5,4},{6,5},{7,6},{8,7},{9,8},{10,9},{11,1... | collective-permute-start | bytes 98312 | tf_op jit(solution)/shard_map/ppermute | solution.py:21
  67.5 1.0 gather_fusion.3
  68.5 9.3 %fusion.21 = f32[16,32,64]{2,0,1:T(8,128)S(1)} fusion(f32[32,8,64,64]{3,2,1,0:T(8,128)} %param.6, f32[32,8,16,64]{3,2,1,0:T(8,128)S(1)} %bitcast.73, pred[32,8]{1,0:T(8,128)(4,1)S(1)} %copy.51), kind=kOutput, calls=%fused_computation.21 | convolution fusion | flops 201588736 | bytes 5374208 | tf_op jit(solution)/shard_map/irkb,rkab->ira/dot_general | solution.py:56
  78.7 18.8 %all-gather = f32[512,64]{1,0:T(8,128)S(1)} all-gather(f32[64,64]{1,0:T(8,128)S(1)} %fusion.32), channel_id=2, replica_groups=mesh['wide_0'=8,'wide_1'=4,'narrow_0'=4,'narrow_1'=2] {'wide_0'}, dimensions={0}, use_global_device_ids=true | all-gather | bytes 147456 | tf_op jit(solution)/shard_map/all_gather | solution.py:34
  97.5 9.1 %all-gather.1 = f32[256,64]{1,0:T(8,128)S(1)} all-gather(f32[64,64]{1,0:T(8,128)S(1)} %reduce_sum.36), channel_id=3, replica_groups=mesh['wide_0'=8,'wide_1'=4,'narrow_0'=4,'narrow_1'=2] {'wide_1'}, dimensions={0}, use_global_device_ids=true | all-gather | bytes 81920 | tf_op jit(solution)/shard_map/all_gather | solution.py:34
  106.6 16.9 %all-gather.2 = f32[256,64]{1,0:T(8,128)S(1)} all-gather(f32[64,64]{1,0:T(8,128)S(1)} %reduce_sum.37), channel_id=4, replica_groups=mesh['wide_0'=8,'wide_1'=4,'narrow_0'=4,'narrow_1'=2] {'narrow_0'}, dimensions={0}, use_global_device_ids=true | all-gather | bytes 81920 | tf_op jit(solution)/shard_map/all_gather | solution.py:34
  123.5 13.7 %all-gather.3 = f32[128,64]{1,0:T(8,128)S(1)} all-gather(f32[64,64]{1,0:T(8,128)S(1)} %reduce_sum.38), channel_id=5, replica_groups=mesh['wide_0'=8,'wide_1'=4,'narrow_0'=4,'narrow_1'=2] {'narrow_1'}, dimensions={0}, use_global_device_ids=true | all-gather | bytes 49152 | tf_op jit(solution)/shard_map/all_gather | solution.py:34
  137.3 5.8 %cholesky.34 = f32[64,64]{1,0:T(8,128)S(1)} custom-call(f32[64,64]{1,0:T(8,128)S(1)} %fusion.46), custom_call_target="Cholesky" | custom-call | tf_op jit(solution)/shard_map/jit(cholesky)/cholesky | solution.py:70
  143.2 0.6 compare_reduce_fusion.1
  143.8 0.7 select_bitcast_fusion
  144.9 4.4 %cholesky.64 = f32[48,48]{1,0:T(8,128)S(1)} custom-call(f32[48,48]{1,0:T(8,128)S(1)} %fusion.53), custom_call_target="Cholesky" | custom-call | tf_op jit(solution)/shard_map/jit(cholesky)/cholesky | solution.py:75
  149.3 0.6 compare_reduce_fusion
  149.9 0.7 fusion.47
  150.6 3.7 %custom-call.11 = f32[1,48,48]{1,2,0:T(8,128)S(1)} custom-call(f32[1,48,48]{2,1,0:T(8,128)S(1)} %fusion.47), custom_call_target="InvertDiagBlocksLowerTriangular" | custom-call | tf_op jit(solution)/shard_map/triangular_solve | solution.py:77
  154.6 1.0 convolution_subtract_fusion
  155.6 1.0 convolution_add_fusion
  (57 shorter events, 5.5 us)
Async XLA Ops:
  1.4 4.3 %collective-permute-start = (f32[16,512]{1,0:T(8,128)S(1)}, f32[16,512]{1,0:T(8,128)S(1)}, u32[]{:S(2)}, u32[]{:S(2)}) collective-permute-start(f32[16,512]{1,0:T(8,128)S(1)} %get-tuple-element.11), channel_id=1, source_target_pairs={{0,1},{1,2},{2,3},{3,4},{4,5},{5,6},{6,7},{7,8},{8,9},{9,10},{10,1... | collective-permute-start | bytes 98312 | tf_op jit(solution)/shard_map/ppermute | solution.py:20
  4.0 3.3 %collective-permute-start.1 = (f32[16,512]{1,0:T(8,128)S(1)}, f32[16,512]{1,0:T(8,128)S(1)}, u32[]{:S(2)}, u32[]{:S(2)}) collective-permute-start(f32[16,512]{1,0:T(8,128)S(1)} %get-tuple-element.12), channel_id=1, source_target_pairs={{1,0},{2,1},{3,2},{4,3},{5,4},{6,5},{7,6},{8,7},{9,8},{10,9},{11,1... | collective-permute-start | bytes 98312 | tf_op jit(solution)/shard_map/ppermute | solution.py:21
  9.6 9.6 %copy-start.1 = (f32[16,2048]{1,0:T(8,128)S(1)}, f32[16,2048]{1,0:T(8,128)}, u32[]{:S(2)}) copy-start(f32[16,2048]{1,0:T(8,128)} %param.8) | copy-start | bytes 393220
  19.2 8.0 %collective-permute-start.2 = (f32[16,512]{1,0:T(8,128)S(1)}, f32[16,512]{1,0:T(8,128)S(1)}, u32[]{:S(2)}, u32[]{:S(2)}) collective-permute-start(f32[16,512]{1,0:T(8,128)S(1)} %get-tuple-element.9), channel_id=1, source_target_pairs={{0,1},{1,2},{2,3},{3,4},{4,5},{5,6},{6,7},{7,8},{8,9},{9,10},{10,1... | collective-permute-start | bytes 98312 | tf_op jit(solution)/shard_map/ppermute | solution.py:20
  19.3 8.1 %collective-permute-start.3 = (f32[16,512]{1,0:T(8,128)S(1)}, f32[16,512]{1,0:T(8,128)S(1)}, u32[]{:S(2)}, u32[]{:S(2)}) collective-permute-start(f32[16,512]{1,0:T(8,128)S(1)} %get-tuple-element.10), channel_id=1, source_target_pairs={{1,0},{2,1},{3,2},{4,3},{5,4},{6,5},{7,6},{8,7},{9,8},{10,9},{11,1... | collective-permute-start | bytes 98312 | tf_op jit(solution)/shard_map/ppermute | solution.py:21
  38.3 8.9 %collective-permute-start.4 = (f32[16,512]{1,0:T(8,128)S(1)}, f32[16,512]{1,0:T(8,128)S(1)}, u32[]{:S(2)}, u32[]{:S(2)}) collective-permute-start(f32[16,512]{1,0:T(8,128)S(1)} %get-tuple-element.7), channel_id=1, source_target_pairs={{0,1},{1,2},{2,3},{3,4},{4,5},{5,6},{6,7},{7,8},{8,9},{9,10},{10,1... | collective-permute-start | bytes 98312 | tf_op jit(solution)/shard_map/ppermute | solution.py:20
  38.6 8.8 %collective-permute-start.5 = (f32[16,512]{1,0:T(8,128)S(1)}, f32[16,512]{1,0:T(8,128)S(1)}, u32[]{:S(2)}, u32[]{:S(2)}) collective-permute-start(f32[16,512]{1,0:T(8,128)S(1)} %get-tuple-element.8), channel_id=1, source_target_pairs={{1,0},{2,1},{3,2},{4,3},{5,4},{6,5},{7,6},{8,7},{9,8},{10,9},{11,1... | collective-permute-start | bytes 98312 | tf_op jit(solution)/shard_map/ppermute | solution.py:21
  58.3 8.7 %collective-permute-start.6 = (f32[16,512]{1,0:T(8,128)S(1)}, f32[16,512]{1,0:T(8,128)S(1)}, u32[]{:S(2)}, u32[]{:S(2)}) collective-permute-start(f32[16,512]{1,0:T(8,128)S(1)} %get-tuple-element.5), channel_id=1, source_target_pairs={{0,1},{1,2},{2,3},{3,4},{4,5},{5,6},{6,7},{7,8},{8,9},{9,10},{10,1... | collective-permute-start | bytes 98312 | tf_op jit(solution)/shard_map/ppermute | solution.py:20
  58.4 8.8 %collective-permute-start.7 = (f32[16,512]{1,0:T(8,128)S(1)}, f32[16,512]{1,0:T(8,128)S(1)}, u32[]{:S(2)}, u32[]{:S(2)}) collective-permute-start(f32[16,512]{1,0:T(8,128)S(1)} %get-tuple-element.6), channel_id=1, source_target_pairs={{1,0},{2,1},{3,2},{4,3},{5,4},{6,5},{7,6},{8,7},{9,8},{10,9},{11,1... | collective-permute-start | bytes 98312 | tf_op jit(solution)/shard_map/ppermute | solution.py:21
  78.1 77.5 %copy-start = (f32[16,2048]{1,0:T(8,128)S(1)}, f32[16,2048]{1,0:T(8,128)}, u32[]{:S(2)}) copy-start(f32[16,2048]{1,0:T(8,128)} %param.9) | copy-start | bytes 393220
